TPU v7x, 256 devices: a whole 4x4x8 slice. The times are simulated.
256 devices in a mesh: sec: 32 (over x, z), op: 8 (over y, core).
Axes of the slice: x: 4, y: 4, z: 8, core: 2. Of those that a mesh axis runs over, the one named last changes fastest.
Arguments:
- state_start: bfloat16 [64, 256, 256], P('sec'), may hold values from -60 to 60
- left_ops: bfloat16 [64, 64, 256, 256], P('op', 'sec'), may hold values from -0.375 to 0.375
- right_ops: bfloat16 [64, 64, 256, 256], P('op', 'sec'), may hold values from -0.046875 to 0.046875
- shift: float32 [64], P('sec'), may hold values from 0.2 to 2.2
- partner: int32 [64, 64], P('op', 'sec'), may hold values from 0 to 5
- kept: int32 [64], P('sec'), may hold values from 128 to 256
Outputs:
- state_final: bfloat16 [64, 256, 256], P('sec')
- new_ops: bfloat16 [64, 64, 256, 256], P('op', 'sec')
Inputs may be any that keep to these rules, and one draw needn't show every extreme that they name: `partner`: position in the window of 6 sector blocks.
All inputs are finite; a program needn't handle non-finite values.
Results may differ from a plain program's by a relative error of at most 0.015.
Values may be sent and summed in bfloat16 or wider, within the bound.
A program may use at most 64 MiB of HBM per device.

v0:
```python
import jax
import jax.numpy as jnp
from jax import lax
from jax.sharding import PartitionSpec as P

ITERS = 4
step_size = 0.5


def padded(cells, sides, width):
    for axis, dim in sides:
        count = lax.axis_size(axis)
        head = lax.slice_in_dim(cells, 0, width, axis=dim)
        tail = lax.slice_in_dim(cells, cells.shape[dim] - width, cells.shape[dim], axis=dim)
        cells = jnp.concatenate(
            [
                lax.ppermute(tail, axis, [(i, (i + 1) % count) for i in range(count)]),
                cells,
                lax.ppermute(head, axis, [((i + 1) % count, i) for i in range(count)]),
            ],
            axis=dim,
        )
    return cells


def shifted(block, axis, distance):
    devices = range(lax.axis_size(axis))
    route = [((i - distance) % len(devices), i) for i in devices]
    return lax.ppermute(block, axis, route)


def per_device(state_start, left_ops, right_ops, shift, partner, kept):
    sector_local = state_start.shape[0]
    width = state_start.shape[1]
    share_rows = width // lax.axis_size("op")
    share_start = lax.axis_index("op") * share_rows
    count = float(sector_local * lax.axis_size("sec") * width * width)
    shift_col = shift[:, None, None]
    state = state_start
    for iteration in range(ITERS):
        window = padded(state, (("sec", 0),), sector_local)
        sources = window[partner]
        halfway = jnp.einsum(
            "tbij,tbjk->tbik", left_ops, sources, preferred_element_type=jnp.float32
        ).astype(jnp.bfloat16)
        partial_sigma = jnp.einsum(
            "tbij,tbjk->bik", halfway, right_ops, preferred_element_type=jnp.float32
        )
        state_wide = state.astype(jnp.float32)
        state_part = lax.dynamic_slice_in_dim(state_wide, share_start, share_rows, 1)
        sigma = lax.psum(partial_sigma, "op") + shift_col * state_wide
        sigma_part = lax.dynamic_slice_in_dim(sigma, share_start, share_rows, 1)
        energy_sum, norm_sum, square_sum = lax.psum(
            (
                jnp.sum(state_part * sigma_part),
                jnp.sum(state_part * state_part),
                jnp.sum(sigma_part * sigma_part),
            ),
            ("sec", "op"),
        )
        ratio = energy_sum / norm_sum
        updated_part = state_part - step_size * (sigma_part - ratio * state_part)
        new_norm = lax.psum(jnp.sum(updated_part * updated_part), ("sec", "op"))
        factor = jnp.sqrt(count / new_norm)
        updated = state_wide - step_size * (sigma - ratio * state_wide)
        state = (updated * factor).astype(jnp.bfloat16)
    columns = jnp.arange(width, dtype=jnp.int32)
    keep_mask = (columns[None, :] < kept[:, None]).astype(jnp.bfloat16)
    kept_block = state * keep_mask[:, None, :]
    out_scale = 1.0 / float(width) ** 0.5
    projected = jnp.einsum(
        "tbij,bjk->tbik", left_ops, kept_block, preferred_element_type=jnp.float32
    ).astype(jnp.bfloat16)
    renormed = (
        jnp.einsum("bji,tbjk->tbik", kept_block, projected, preferred_element_type=jnp.float32)
        * out_scale
    ).astype(jnp.bfloat16)
    new_ops = shifted(renormed, "sec", 1)
    return (state, new_ops)


def solution(mesh):
    in_specs = (
        P("sec", None, None),
        P("op", "sec", None, None),
        P("op", "sec", None, None),
        P("sec"),
        P("op", "sec"),
        P("sec"),
    )
    out_specs = (P("sec", None, None), P("op", "sec", None, None))
    return jax.shard_map(
        per_device, mesh=mesh, in_specs=in_specs, out_specs=out_specs, check_vma=False
    )
```

profile of v0, /device:TPU:1, one launch (start us, length us, event | category | flops | bytes accessed | tf_op | source)
XLA Modules:
  0.0 1021.9 jit_solution(1389676207874550599)
XLA Ops:
  7.2 2.5 collective-permute-start
  9.8 6.2 collective-permute-start.1
  16.9 5.3 collective-permute-done
  22.1 1.0 pad_maximum_fusion
  23.2 2.0 gather_fusion
  25.2 4.3 fusion.47
  30.5 62.1 %all-reduce.9.cloned.1.call-done = f32[2,256,256]{2,1,0:T(8,128)} async-done(((f32[2,256,256]{2,1,0:T(8,128)}), f32[2,256,256]{2,1,0:T(8,128)}) %all-reduce.9.cloned.1.call-update) | async-done | bytes 524304 | tf_op jit(solution)/shard_map/psum | solution.py:51
  92.6 1.2 multiply_add_fusion.3
  93.7 1.6 multiply_reduce_fusion.10
  95.3 78.5 %all-reduce.3 = (f32[]{:T(128)}, f32[]{:T(128)}) all-reduce(f32[]{:T(128)} %get-tuple-element.13, f32[]{:T(128)} %get-tuple-element.12), channel_id=1, replica_groups=mesh['sec'=32,'op'=8] {'sec','op'}, use_global_device_ids=true, to_apply=%region_2.0 | all-reduce | flops 2 | bytes 16 | tf_op jit(solution)/shard_map/psum | solution.py:53
  175.0 1.5 multiply_reduce_fusion.9
  176.5 73.4 %psum.115 = f32[]{:T(128)} all-reduce(f32[]{:T(128)} %multiply_reduce_fusion.9), channel_id=1, replica_groups=mesh['sec'=32,'op'=8] {'sec','op'}, use_global_device_ids=true, to_apply=%region_6.0 | all-reduce | flops 1 | bytes 8 | tf_op jit(solution)/shard_map/psum | solution.py:63
  251.6 2.2 collective-permute-start.3
  253.7 5.0 collective-permute-done.3
  258.8 5.2 collective-permute-done.2
  264.0 2.0 gather_fusion.1
  266.0 4.3 fusion.54
  270.4 57.5 %all-reduce.11.cloned.1.call-done = f32[2,256,256]{2,1,0:T(8,128)} async-done(((f32[2,256,256]{2,1,0:T(8,128)}), f32[2,256,256]{2,1,0:T(8,128)}) %all-reduce.11.cloned.1.call-update) | async-done | bytes 524304 | tf_op jit(solution)/shard_map/psum | solution.py:51
  327.9 1.2 multiply_add_fusion.2
  329.1 1.5 multiply_reduce_fusion.7
  330.6 78.5 %all-reduce.2 = (f32[]{:T(128)}, f32[]{:T(128)}) all-reduce(f32[]{:T(128)} %get-tuple-element.11, f32[]{:T(128)} %get-tuple-element.10), channel_id=1, replica_groups=mesh['sec'=32,'op'=8] {'sec','op'}, use_global_device_ids=true, to_apply=%region_9.0 | all-reduce | flops 2 | bytes 16 | tf_op jit(solution)/shard_map/psum | solution.py:53
  410.4 1.5 multiply_reduce_fusion.6
  411.9 73.4 %psum.119 = f32[]{:T(128)} all-reduce(f32[]{:T(128)} %multiply_reduce_fusion.6), channel_id=1, replica_groups=mesh['sec'=32,'op'=8] {'sec','op'}, use_global_device_ids=true, to_apply=%region_13.0 | all-reduce | flops 1 | bytes 8 | tf_op jit(solution)/shard_map/psum | solution.py:63
  486.9 2.2 collective-permute-start.5
  489.1 5.0 collective-permute-done.5
  494.1 5.2 collective-permute-done.4
  499.4 2.0 gather_fusion.2
  501.4 4.3 fusion.61
  505.8 57.6 %all-reduce.13.cloned.1.call-done = f32[2,256,256]{2,1,0:T(8,128)} async-done(((f32[2,256,256]{2,1,0:T(8,128)}), f32[2,256,256]{2,1,0:T(8,128)}) %all-reduce.13.cloned.1.call-update) | async-done | bytes 524304 | tf_op jit(solution)/shard_map/psum | solution.py:51
  563.3 1.2 multiply_add_fusion.1
  564.5 1.5 multiply_reduce_fusion.4
  566.0 78.5 %all-reduce.1 = (f32[]{:T(128)}, f32[]{:T(128)}) all-reduce(f32[]{:T(128)} %get-tuple-element.9, f32[]{:T(128)} %get-tuple-element.8), channel_id=1, replica_groups=mesh['sec'=32,'op'=8] {'sec','op'}, use_global_device_ids=true, to_apply=%region_16.0 | all-reduce | flops 2 | bytes 16 | tf_op jit(solution)/shard_map/psum | solution.py:53
  645.8 1.5 multiply_reduce_fusion.3
  647.3 73.4 %psum.123 = f32[]{:T(128)} all-reduce(f32[]{:T(128)} %multiply_reduce_fusion.3), channel_id=1, replica_groups=mesh['sec'=32,'op'=8] {'sec','op'}, use_global_device_ids=true, to_apply=%region_20.0 | all-reduce | flops 1 | bytes 8 | tf_op jit(solution)/shard_map/psum | solution.py:63
  722.3 2.2 collective-permute-start.7
  724.5 5.0 collective-permute-done.7
  729.5 5.2 collective-permute-done.6
  734.8 2.0 gather_fusion.3
  736.8 4.3 fusion.68
  741.1 57.6 %all-reduce.15.cloned.1.call-done = f32[2,256,256]{2,1,0:T(8,128)} async-done(((f32[2,256,256]{2,1,0:T(8,128)}), f32[2,256,256]{2,1,0:T(8,128)}) %all-reduce.15.cloned.1.call-update) | async-done | bytes 524304 | tf_op jit(solution)/shard_map/psum | solution.py:51
  798.7 1.2 multiply_add_fusion
  799.9 1.5 multiply_reduce_fusion.1
  801.4 78.5 %all-reduce = (f32[]{:T(128)}, f32[]{:T(128)}) all-reduce(f32[]{:T(128)} %get-tuple-element.7, f32[]{:T(128)} %get-tuple-element.6), channel_id=1, replica_groups=mesh['sec'=32,'op'=8] {'sec','op'}, use_global_device_ids=true, to_apply=%region_23.0 | all-reduce | flops 2 | bytes 16 | tf_op jit(solution)/shard_map/psum | solution.py:53
  881.2 1.5 multiply_reduce_fusion
  882.7 73.4 %psum.127 = f32[]{:T(128)} all-reduce(f32[]{:T(128)} %multiply_reduce_fusion), channel_id=1, replica_groups=mesh['sec'=32,'op'=8] {'sec','op'}, use_global_device_ids=true, to_apply=%region_27.0 | all-reduce | flops 1 | bytes 8 | tf_op jit(solution)/shard_map/psum | solution.py:63
  957.0 4.3 fusion.40
  962.3 49.2 %collective-permute-done.8 = bf16[8,2,256,256]{2,3,0,1:T(8,128)(2,1)} collective-permute-done((bf16[8,2,256,256]{2,3,0,1:T(8,128)(2,1)}, bf16[8,2,256,256]{2,3,0,1:T(8,128)(2,1)}, u32[]{:S(2)}, u32[]{:S(2)}) %collective-permute-start.8) | collective-permute-done | bytes 2097184 | tf_op jit(solution)/shard_map/ppermute | solution.py:29
  1011.5 3.9 copy.19
  (36 shorter events, 6.0 us)
Async XLA Ops:
  7.2 18.0 %copy-start = (bf16[8,2,256,256]{3,2,1,0:T(8,128)(2,1)S(1)}, bf16[8,2,256,256]{3,2,1,0:T(8,128)(2,1)}, u32[]{:S(2)}) copy-start(bf16[8,2,256,256]{3,2,1,0:T(8,128)(2,1)} %param.8) | copy-start | bytes 6291460
  7.2 85.4 %all-reduce.9.cloned.1.call-start = ((), (), s32[]{:S(2)}) async-start(), calls=%async_computation | async-start | bytes 1048576 | tf_op jit(solution)/shard_map/psum | solution.py:51
  7.2 14.9 %collective-permute-start = (bf16[2,256,256]{2,1,0:T(8,128)(2,1)}, bf16[2,256,256]{2,1,0:T(8,128)(2,1)S(1)}, u32[]{:S(2)}, u32[]{:S(2)}) collective-permute-start(bf16[2,256,256]{2,1,0:T(8,128)(2,1)} %param.6), channel_id=1, source_target_pairs={{0,8},{8,16},{16,24},{24,32},{32,40},{40,48},{48,56},{56,64},{64,7... | collective-permute-start | bytes 786440 | tf_op jit(solution)/shard_map/ppermute | solution.py:17
  9.8 12.4 %collective-permute-start.1 = (bf16[2,256,256]{2,1,0:T(8,128)(2,1)}, bf16[2,256,256]{2,1,0:T(8,128)(2,1)S(1)}, u32[]{:S(2)}, u32[]{:S(2)}) collective-permute-start(bf16[2,256,256]{2,1,0:T(8,128)(2,1)} %param.6), channel_id=1, source_target_pairs={{8,0},{16,8},{24,16},{32,24},{40,32},{48,40},{56,48},{64,56},{72,6... | collective-permute-start | bytes 786440 | tf_op jit(solution)/shard_map/ppermute | solution.py:19
  25.2 4.4 copy-start.1
  25.2 67.4 %copy-start.3 = (f32[2]{0:T(128)S(1)}, f32[2]{0:T(128)}, u32[]{:S(2)}) copy-start(f32[2]{0:T(128)} %param.9) | copy-start | bytes 28
  29.6 298.4 %all-reduce.11.cloned.1.call-start = ((), (), s32[]{:S(2)}) async-start(), calls=%async_computation.1 | async-start | bytes 1048576 | tf_op jit(solution)/shard_map/psum | solution.py:51
  251.6 7.2 collective-permute-start.3
  253.7 10.2 collective-permute-start.2
  270.3 293.0 %all-reduce.13.cloned.1.call-start = ((), (), s32[]{:S(2)}) async-start(), calls=%async_computation.2 | async-start | bytes 1048576 | tf_op jit(solution)/shard_map/psum | solution.py:51
  486.9 7.2 collective-permute-start.5
  489.1 10.2 collective-permute-start.4
  505.7 293.0 %all-reduce.15.cloned.1.call-start = ((), (), s32[]{:S(2)}) async-start(), calls=%async_computation.3 | async-start | bytes 1048576 | tf_op jit(solution)/shard_map/psum | solution.py:51
  722.3 7.2 collective-permute-start.7
  724.5 10.2 collective-permute-start.6
  741.1 141.5 %copy-start.4 = (s32[2]{0:T(128)S(1)}, s32[2]{0:T(128)}, u32[]{:S(2)}) copy-start(s32[2]{0:T(128)} %param.11) | copy-start | bytes 28
  957.0 4.3 copy-start.2
  961.3 50.2 %collective-permute-start.8 = (bf16[8,2,256,256]{2,3,0,1:T(8,128)(2,1)}, bf16[8,2,256,256]{2,3,0,1:T(8,128)(2,1)}, u32[]{:S(2)}, u32[]{:S(2)}) collective-permute-start(bf16[8,2,256,256]{2,3,0,1:T(8,128)(2,1)} %fusion.40), channel_id=1, source_target_pairs={{248,0},{0,8},{8,16},{16,24},{24,32},{32,40},{40,48},{48,56},{56,6... | collective-permute-start | bytes 6291464 | tf_op jit(solution)/shard_map/ppermute | solution.py:29
Sparse Core Ops, SparseCore 0:
  29.7 62.8 all-reduce.8
  270.5 57.4 all-reduce.10
  505.8 57.4 all-reduce.12
  741.2 57.4 all-reduce.14
where the time goes:
time: 1020 us
  blocking collectives  608 us (60%)
  waiting for transfers between devices  320 us (31%)
  other arithmetic  22.3 us (2%)
  between operations  22.1 us (2%)
  matrix products  21.6 us (2%)
  starting transfers between devices  16.4 us (2%)
  local copies, waits for them, and re-layouts  12.1 us (1%)
    psum x4, blocking collectives, per_device(): lax.psum((jnp.sum(state_part * sigma_part), jnp.sum(state_part * state_pa...  314 us
    psum x4, blocking collectives, per_device(): new_norm = lax.psum(jnp.sum(updated_part * updated_part), ('sec', 'op'))  294 us
    psum x4, waiting for transfers between devices, per_device(): sigma = lax.psum(partial_sigma, 'op') + shift_col * state_wide  235 us
    ppermute x1, waiting for transfers between devices, shifted(): return lax.ppermute(block, axis, route)  49.2 us
    ppermute x4, waiting for transfers between devices, padded(): lax.ppermute(tail, axis, [(i, (i + 1) % count) for i in range(count)])  20.8 us
  transfers between devices with their start and end apart: 13, of which 12 were waited for; matrix products, arithmetic and copies ran while one was open for 0% of the time, Pallas kernels for 0%

commit v1 on v0

--- a/solution.py
+++ b/solution.py
@@ -5,6 +5,11 @@
 
 ITERS = 4
 step_size = 0.5
+
+
+def by_each_axis(x, axis_one, axis_two):
+    partial = lax.psum(x, axis_one)
+    return lax.psum(partial, axis_two)
 
 
 def padded(cells, sides, width):
@@ -50,13 +55,14 @@
         state_part = lax.dynamic_slice_in_dim(state_wide, share_start, share_rows, 1)
         sigma = lax.psum(partial_sigma, "op") + shift_col * state_wide
         sigma_part = lax.dynamic_slice_in_dim(sigma, share_start, share_rows, 1)
-        energy_sum, norm_sum, square_sum = lax.psum(
+        energy_sum, norm_sum, square_sum = by_each_axis(
             (
                 jnp.sum(state_part * sigma_part),
                 jnp.sum(state_part * state_part),
                 jnp.sum(sigma_part * sigma_part),
             ),
-            ("sec", "op"),
+            "sec",
+            "op",
         )
         ratio = energy_sum / norm_sum
         updated_part = state_part - step_size * (sigma_part - ratio * state_part)

time: 1020 us -> 1070 us (1.049)
  blocking collectives: 608 us -> 654 us
    psum x4 -> x8, blocking collectives: 314 us -> 363 us  [the longest x4 247 us: by_each_axis(): partial = lax.psum(x, axis_one)]
where the time goes in v1:
time: 1070 us
  blocking collectives  654 us (61%)
  waiting for transfers between devices  317 us (30%)
  other arithmetic  22.2 us (2%)
  between operations  22.1 us (2%)
  matrix products  21.6 us (2%)
  starting transfers between devices  18.2 us (2%)
  local copies, waits for them, and re-layouts  12.1 us (1%)
    psum x4, blocking collectives, per_device(): new_norm = lax.psum(jnp.sum(updated_part * updated_part), ('sec', 'op'))  290 us
    psum x4, blocking collectives, by_each_axis(): partial = lax.psum(x, axis_one)  247 us
    psum x4, waiting for transfers between devices, per_device(): sigma = lax.psum(partial_sigma, 'op') + shift_col * state_wide  233 us
    psum x4, blocking collectives, by_each_axis(): return lax.psum(partial, axis_two)  116 us
    ppermute x1, waiting for transfers between devices, shifted(): return lax.ppermute(block, axis, route)  48.4 us
  transfers between devices with their start and end apart: 13, of which 12 were waited for; matrix products, arithmetic and copies ran while one was open for 0% of the time, Pallas kernels for 0%

profile of v1, /device:TPU:1, one launch (start us, length us, event | category | flops | bytes accessed | tf_op | source)
XLA Modules:
  0.0 1066.6 jit_solution(4058062092823648857)
XLA Ops:
  7.2 2.5 collective-permute-start
  9.8 6.2 collective-permute-start.1
  16.9 5.3 collective-permute-done
  23.2 2.0 gather_fusion
  25.2 4.3 fusion.47
  30.5 62.1 %all-reduce.13.cloned.1.call-done = f32[2,256,256]{2,1,0:T(8,128)} async-done(((f32[2,256,256]{2,1,0:T(8,128)}), f32[2,256,256]{2,1,0:T(8,128)}) %all-reduce.13.cloned.1.call-update) | async-done | bytes 524304 | tf_op jit(solution)/shard_map/psum | solution.py:56
  93.7 1.5 multiply_reduce_fusion.10
  95.2 61.7 %all-reduce.3 = (f32[]{:T(128)}, f32[]{:T(128)}) all-reduce(f32[]{:T(128)} %get-tuple-element.13, f32[]{:T(128)} %get-tuple-element.12), channel_id=1, replica_groups=mesh['sec'=32,'op'=8] {'sec'}, use_global_device_ids=true, to_apply=%region_2.0 | all-reduce | flops 2 | bytes 16 | tf_op jit(solution)/shard_map/psum | solution.py:11
  156.9 29.1 %all-reduce.7 = (f32[]{:T(128)}, f32[]{:T(128)}) all-reduce(f32[]{:T(128)} %get-tuple-element.20, f32[]{:T(128)} %get-tuple-element.21), channel_id=1, replica_groups=mesh['sec'=32,'op'=8] {'op'}, use_global_device_ids=true, to_apply=%region_3.0 | all-reduce | flops 2 | bytes 16 | tf_op jit(solution)/shard_map/psum | solution.py:12
  187.3 1.5 multiply_reduce_fusion.9
  188.8 72.6 %psum.173 = f32[]{:T(128)} all-reduce(f32[]{:T(128)} %multiply_reduce_fusion.9), channel_id=1, replica_groups=mesh['sec'=32,'op'=8] {'sec','op'}, use_global_device_ids=true, to_apply=%region_8.0 | all-reduce | flops 1 | bytes 8 | tf_op jit(solution)/shard_map/psum | solution.py:69
  263.0 2.5 collective-permute-start.3
  265.5 5.3 collective-permute-done.3
  270.8 4.9 collective-permute-done.2
  275.8 2.0 gather_fusion.1
  277.8 4.3 fusion.54
  282.2 56.8 %all-reduce.15.cloned.1.call-done = f32[2,256,256]{2,1,0:T(8,128)} async-done(((f32[2,256,256]{2,1,0:T(8,128)}), f32[2,256,256]{2,1,0:T(8,128)}) %all-reduce.15.cloned.1.call-update) | async-done | bytes 524304 | tf_op jit(solution)/shard_map/psum | solution.py:56
  340.1 1.5 multiply_reduce_fusion.7
  341.6 61.6 %all-reduce.2 = (f32[]{:T(128)}, f32[]{:T(128)}) all-reduce(f32[]{:T(128)} %get-tuple-element.11, f32[]{:T(128)} %get-tuple-element.10), channel_id=1, replica_groups=mesh['sec'=32,'op'=8] {'sec'}, use_global_device_ids=true, to_apply=%region_11.0 | all-reduce | flops 2 | bytes 16 | tf_op jit(solution)/shard_map/psum | solution.py:11
  403.3 29.1 %all-reduce.6 = (f32[]{:T(128)}, f32[]{:T(128)}) all-reduce(f32[]{:T(128)} %get-tuple-element.18, f32[]{:T(128)} %get-tuple-element.19), channel_id=1, replica_groups=mesh['sec'=32,'op'=8] {'op'}, use_global_device_ids=true, to_apply=%region_12.0 | all-reduce | flops 2 | bytes 16 | tf_op jit(solution)/shard_map/psum | solution.py:12
  433.7 1.5 multiply_reduce_fusion.6
  435.2 72.6 %psum.179 = f32[]{:T(128)} all-reduce(f32[]{:T(128)} %multiply_reduce_fusion.6), channel_id=1, replica_groups=mesh['sec'=32,'op'=8] {'sec','op'}, use_global_device_ids=true, to_apply=%region_17.0 | all-reduce | flops 1 | bytes 8 | tf_op jit(solution)/shard_map/psum | solution.py:69
  509.4 2.5 collective-permute-start.5
  511.9 5.3 collective-permute-done.5
  517.2 4.9 collective-permute-done.4
  522.2 2.0 gather_fusion.2
  524.2 4.3 fusion.61
  528.6 56.8 %all-reduce.17.cloned.1.call-done = f32[2,256,256]{2,1,0:T(8,128)} async-done(((f32[2,256,256]{2,1,0:T(8,128)}), f32[2,256,256]{2,1,0:T(8,128)}) %all-reduce.17.cloned.1.call-update) | async-done | bytes 524304 | tf_op jit(solution)/shard_map/psum | solution.py:56
  586.5 1.5 multiply_reduce_fusion.4
  588.0 61.8 %all-reduce.1 = (f32[]{:T(128)}, f32[]{:T(128)}) all-reduce(f32[]{:T(128)} %get-tuple-element.9, f32[]{:T(128)} %get-tuple-element.8), channel_id=1, replica_groups=mesh['sec'=32,'op'=8] {'sec'}, use_global_device_ids=true, to_apply=%region_20.0 | all-reduce | flops 2 | bytes 16 | tf_op jit(solution)/shard_map/psum | solution.py:11
  649.8 29.1 %all-reduce.5 = (f32[]{:T(128)}, f32[]{:T(128)}) all-reduce(f32[]{:T(128)} %get-tuple-element.16, f32[]{:T(128)} %get-tuple-element.17), channel_id=1, replica_groups=mesh['sec'=32,'op'=8] {'op'}, use_global_device_ids=true, to_apply=%region_21.0 | all-reduce | flops 2 | bytes 16 | tf_op jit(solution)/shard_map/psum | solution.py:12
  680.3 1.5 multiply_reduce_fusion.3
  681.8 72.6 %psum.185 = f32[]{:T(128)} all-reduce(f32[]{:T(128)} %multiply_reduce_fusion.3), channel_id=1, replica_groups=mesh['sec'=32,'op'=8] {'sec','op'}, use_global_device_ids=true, to_apply=%region_26.0 | all-reduce | flops 1 | bytes 8 | tf_op jit(solution)/shard_map/psum | solution.py:69
  756.0 2.5 collective-permute-start.7
  758.5 5.3 collective-permute-done.7
  763.8 4.9 collective-permute-done.6
  768.8 2.0 gather_fusion.3
  770.8 4.3 fusion.68
  775.1 56.8 %all-reduce.19.cloned.1.call-done = f32[2,256,256]{2,1,0:T(8,128)} async-done(((f32[2,256,256]{2,1,0:T(8,128)}), f32[2,256,256]{2,1,0:T(8,128)}) %all-reduce.19.cloned.1.call-update) | async-done | bytes 524304 | tf_op jit(solution)/shard_map/psum | solution.py:56
  833.1 1.5 multiply_reduce_fusion.1
  834.6 61.6 %all-reduce = (f32[]{:T(128)}, f32[]{:T(128)}) all-reduce(f32[]{:T(128)} %get-tuple-element.7, f32[]{:T(128)} %get-tuple-element.6), channel_id=1, replica_groups=mesh['sec'=32,'op'=8] {'sec'}, use_global_device_ids=true, to_apply=%region_29.0 | all-reduce | flops 2 | bytes 16 | tf_op jit(solution)/shard_map/psum | solution.py:11
  896.3 29.1 %all-reduce.4 = (f32[]{:T(128)}, f32[]{:T(128)}) all-reduce(f32[]{:T(128)} %get-tuple-element.14, f32[]{:T(128)} %get-tuple-element.15), channel_id=1, replica_groups=mesh['sec'=32,'op'=8] {'op'}, use_global_device_ids=true, to_apply=%region_30.0 | all-reduce | flops 2 | bytes 16 | tf_op jit(solution)/shard_map/psum | solution.py:12
  926.7 1.5 multiply_reduce_fusion
  928.3 72.6 %psum.191 = f32[]{:T(128)} all-reduce(f32[]{:T(128)} %multiply_reduce_fusion), channel_id=1, replica_groups=mesh['sec'=32,'op'=8] {'sec','op'}, use_global_device_ids=true, to_apply=%region_35.0 | all-reduce | flops 1 | bytes 8 | tf_op jit(solution)/shard_map/psum | solution.py:69
  1001.7 4.3 fusion.40
  1006.0 1.8 collective-permute-start.8
  1007.8 48.4 %collective-permute-done.8 = bf16[8,2,256,256]{2,3,0,1:T(8,128)(2,1)} collective-permute-done((bf16[8,2,256,256]{2,3,0,1:T(8,128)(2,1)}, bf16[8,2,256,256]{2,3,0,1:T(8,128)(2,1)}, u32[]{:S(2)}, u32[]{:S(2)}) %collective-permute-start.8) | collective-permute-done | bytes 2097184 | tf_op jit(solution)/shard_map/ppermute | solution.py:34
  1056.2 3.9 copy.19
  (40 shorter events, 10.8 us)
Async XLA Ops:
  7.2 18.0 %copy-start = (bf16[8,2,256,256]{3,2,1,0:T(8,128)(2,1)S(1)}, bf16[8,2,256,256]{3,2,1,0:T(8,128)(2,1)}, u32[]{:S(2)}) copy-start(bf16[8,2,256,256]{3,2,1,0:T(8,128)(2,1)} %param.8) | copy-start | bytes 6291460
  7.2 85.4 %all-reduce.13.cloned.1.call-start = ((), (), s32[]{:S(2)}) async-start(), calls=%async_computation | async-start | bytes 1048576 | tf_op jit(solution)/shard_map/psum | solution.py:56
  7.2 14.9 %collective-permute-start = (bf16[2,256,256]{2,1,0:T(8,128)(2,1)}, bf16[2,256,256]{2,1,0:T(8,128)(2,1)S(1)}, u32[]{:S(2)}, u32[]{:S(2)}) collective-permute-start(bf16[2,256,256]{2,1,0:T(8,128)(2,1)} %param.6), channel_id=1, source_target_pairs={{0,8},{8,16},{16,24},{24,32},{32,40},{40,48},{48,56},{56,64},{64,7... | collective-permute-start | bytes 786440 | tf_op jit(solution)/shard_map/ppermute | solution.py:22
  9.8 12.4 %collective-permute-start.1 = (bf16[2,256,256]{2,1,0:T(8,128)(2,1)}, bf16[2,256,256]{2,1,0:T(8,128)(2,1)S(1)}, u32[]{:S(2)}, u32[]{:S(2)}) collective-permute-start(bf16[2,256,256]{2,1,0:T(8,128)(2,1)} %param.6), channel_id=1, source_target_pairs={{8,0},{16,8},{24,16},{32,24},{40,32},{48,40},{56,48},{64,56},{72,6... | collective-permute-start | bytes 786440 | tf_op jit(solution)/shard_map/ppermute | solution.py:24
  25.2 4.4 copy-start.1
  25.2 67.4 %copy-start.3 = (f32[2]{0:T(128)S(1)}, f32[2]{0:T(128)}, u32[]{:S(2)}) copy-start(f32[2]{0:T(128)} %param.9) | copy-start | bytes 28
  29.6 309.4 %all-reduce.15.cloned.1.call-start = ((), (), s32[]{:S(2)}) async-start(), calls=%async_computation.1 | async-start | bytes 1048576 | tf_op jit(solution)/shard_map/psum | solution.py:56
  263.0 7.8 collective-permute-start.3
  265.5 10.2 collective-permute-start.2
  282.1 303.3 %all-reduce.17.cloned.1.call-start = ((), (), s32[]{:S(2)}) async-start(), calls=%async_computation.2 | async-start | bytes 1048576 | tf_op jit(solution)/shard_map/psum | solution.py:56
  509.4 7.8 collective-permute-start.5
  511.9 10.2 collective-permute-start.4
  528.5 303.4 %all-reduce.19.cloned.1.call-start = ((), (), s32[]{:S(2)}) async-start(), calls=%async_computation.3 | async-start | bytes 1048576 | tf_op jit(solution)/shard_map/psum | solution.py:56
  756.0 7.8 collective-permute-start.7
  758.5 10.2 collective-permute-start.6
  775.1 153.1 %copy-start.4 = (s32[2]{0:T(128)S(1)}, s32[2]{0:T(128)}, u32[]{:S(2)}) copy-start(s32[2]{0:T(128)} %param.11) | copy-start | bytes 28
  1001.7 4.3 copy-start.2
  1006.0 50.2 %collective-permute-start.8 = (bf16[8,2,256,256]{2,3,0,1:T(8,128)(2,1)}, bf16[8,2,256,256]{2,3,0,1:T(8,128)(2,1)}, u32[]{:S(2)}, u32[]{:S(2)}) collective-permute-start(bf16[8,2,256,256]{2,3,0,1:T(8,128)(2,1)} %fusion.40), channel_id=1, source_target_pairs={{248,0},{0,8},{8,16},{16,24},{24,32},{32,40},{40,48},{48,56},{56,6... | collective-permute-start | bytes 6291464 | tf_op jit(solution)/shard_map/ppermute | solution.py:34
Sparse Core Ops, SparseCore 0:
  29.7 62.8 all-reduce.12
  282.2 56.6 all-reduce.14
  528.7 56.6 all-reduce.16
  775.2 56.6 all-reduce.18
